TPU v7x, 32 devices: a whole 2x2x4 slice. The times are simulated.
32 devices in a mesh: row: 2 (over x), col: 16 (over z, y, core).
Axes of the slice: x: 2, y: 2, z: 4, core: 2. Of those that a mesh axis runs over, the one named last changes fastest.
Arguments:
- query_proj: bfloat16 [16384, 4096], P(('col', 'row')), may hold values from -9 to 9
- key_proj: bfloat16 [16384, 512], P(('col', 'row')), may hold values from -9 to 9
- value_proj: bfloat16 [16384, 512], P(('col', 'row')), may hold values from -6 to 6
- segment_ids: int32 [16, 1024], P('col'), may hold values from 0 to 3, never falling along the last dimension, each value on 1 to 512 neighbouring positions
- out_weight: bfloat16 [4096, 8192], P('col', 'row'), may hold values from -0.09375 to 0.09375
- residual: bfloat16 [16384, 8192], P('col', 'row'), may hold values from -4 to 4
- norm_gain: float32 [8192], P('row'), may hold values from 0.1 to 1.9
Outputs:
- residual_sum: bfloat16 [16384, 8192], P('col', 'row')
- normed: bfloat16 [16384, 8192], P('col', 'row')
Inputs may be any that keep to these rules, and one draw needn't show every extreme that they name: `segment_ids`: along each packed sequence the document number never falls; each document spans at most 512 positions and one spans exactly that.
All inputs are finite; a program needn't handle non-finite values.
Results may differ from a plain program's by a relative error of at most 0.0044.
Values may be sent and summed in bfloat16 or wider, within the bound.
A program may use at most 192 MiB of HBM per device.

v0:
```python
import jax
import jax.numpy as jnp
from jax import lax
from jax.sharding import PartitionSpec as P

D = 8192
HD = 128
HK = 4


def attend_local(query_heads, key_heads, value_heads, segment_row):
    length = query_heads.shape[0]
    kv_local = key_heads.shape[1] // HD
    group = query_heads.shape[1] // HD // kv_local
    query_grid = query_heads.reshape(length, kv_local, group, HD).transpose(1, 2, 0, 3)
    key_grid = key_heads.reshape(length, kv_local, HD).transpose(1, 0, 2)
    value_grid = value_heads.reshape(length, kv_local, HD).transpose(1, 0, 2)
    places = jnp.arange(length)
    allowed = (segment_row[:, None] == segment_row[None, :]) & (places[None, :] <= places[:, None])

    def one_group(operands):
        group_query, group_key, group_value = operands
        scores = jnp.einsum(
            "gqd,kd->gqk", group_query, group_key, preferred_element_type=jnp.float32
        ) * HD ** (-0.5)
        scores = jnp.where(allowed, scores, jnp.float32(-1e30))
        peak = jnp.max(scores, axis=-1, keepdims=True)
        weights = jnp.where(allowed, jnp.exp(scores - peak), jnp.float32(0.0))
        totals = jnp.sum(weights, axis=-1, keepdims=True)
        probs = weights.astype(jnp.bfloat16)
        mixture = (
            jnp.einsum("gqk,kd->gqd", probs, group_value, preferred_element_type=jnp.float32)
            / totals
        )
        return mixture.astype(jnp.bfloat16)

    heads_out = lax.map(one_group, (query_grid, key_grid, value_grid))
    return heads_out.transpose(2, 0, 1, 3).reshape(length, kv_local * group * HD)


def widen_heads(proj_rows, repeat):
    rows_local = proj_rows.shape[0]
    kv_count = proj_rows.shape[1] // HD
    if repeat == 1:
        return proj_rows
    spread = jnp.broadcast_to(
        proj_rows.reshape(rows_local, kv_count, 1, HD), (rows_local, kv_count, repeat, HD)
    )
    return spread.reshape(rows_local, kv_count * repeat * HD)


def body(query_proj, key_proj, value_proj, segment_ids, out_weight, residual, norm_gain):
    row_count = lax.axis_size("row")
    repeat = max(row_count // HK, 1)
    key_wide = widen_heads(key_proj, repeat)
    value_wide = widen_heads(value_proj, repeat)
    query_heads, key_heads, value_heads = (
        lax.all_to_all(query_proj, "row", split_axis=1, concat_axis=0, tiled=True),
        lax.all_to_all(key_wide, "row", split_axis=1, concat_axis=0, tiled=True),
        lax.all_to_all(value_wide, "row", split_axis=1, concat_axis=0, tiled=True),
    )
    attn = attend_local(query_heads, key_heads, value_heads, segment_ids[0])
    panel_rows = lax.all_gather(attn, "row", axis=1, tiled=True)
    projected = jnp.dot(
        panel_rows,
        lax.all_gather(out_weight, "col", axis=0, tiled=True),
        preferred_element_type=jnp.float32,
    )
    hidden_sum = residual.astype(jnp.float32) + projected
    squares = lax.psum(jnp.sum(hidden_sum * hidden_sum, axis=1), "row")
    scaled = lax.rsqrt(squares / D + jnp.float32(1e-05))
    normed = hidden_sum * scaled[:, None] * norm_gain[None, :]
    return (hidden_sum.astype(jnp.bfloat16), normed.astype(jnp.bfloat16))


def solution(mesh):
    placed = (
        P(("col", "row"), None),
        P(("col", "row"), None),
        P(("col", "row"), None),
        P("col", None),
        P("col", "row"),
        P("col", "row"),
        P("row"),
    )
    return jax.shard_map(
        body,
        mesh=mesh,
        in_specs=placed,
        out_specs=(P("col", "row"), P("col", "row")),
        check_vma=False,
    )
```

profile of v0, /device:TPU:0, one launch (start us, length us, event | category | flops | bytes accessed | tf_op | source)
XLA Modules:
  0.0 514.9 jit_solution(6233350073334996084)
XLA Ops:
  7.2 1.9 copy.42
  9.0 4.2 all-to-all-start.1
  13.2 1.9 copy.41
  15.1 6.9 %all-to-all-done.1 = bf16[512,2,256]{2,0,1:T(8,128)(2,1)S(1)} async-done(((bf16[512,2,256]{2,0,1:T(8,128)(2,1)}), bf16[512,2,256]{2,0,1:T(8,128)(2,1)S(1)}, u32[]{:S(2)}, u32[]{:S(2)}) %all-to-all-start.1) | async-done | bytes 524320 | tf_op jit(solution)/shard_map/all_to_all | solution.py:59
  22.0 3.5 all-to-all-start.2
  25.5 4.8 copy.40
  30.3 2.9 all-to-all-done.2
  33.1 5.6 %all-to-all-start = ((bf16[512,2,2048]{2,0,1:T(8,128)(2,1)}), bf16[512,2,2048]{2,0,1:T(8,128)(2,1)}, u32[]{:S(2)}, u32[]{:S(2)}) async-start(bf16[512,2,2048]{2,0,1:T(8,128)(2,1)} %bitcast.71), calls=%async_computation | async-start | bytes 8388608 | tf_op jit(solution)/shard_map/all_to_all | solution.py:58
  38.8 0.0 copy-start
  38.8 0.0 all-gather.3.cloned.1.call-start
  38.8 0.1 reshape.34
  39.0 0.9 copy.15
  39.8 0.1 reshape.35
  40.0 0.9 copy.16
  40.9 44.1 %all-to-all-done = bf16[512,2,2048]{2,0,1:T(8,128)(2,1)} async-done(((bf16[512,2,2048]{2,0,1:T(8,128)(2,1)}), bf16[512,2,2048]{2,0,1:T(8,128)(2,1)}, u32[]{:S(2)}, u32[]{:S(2)}) %all-to-all-start) | async-done | bytes 4194336 | tf_op jit(solution)/shard_map/all_to_all | solution.py:58
  85.0 5.6 %copy.25 = bf16[128,8,16,128]{3,2,1,0:T(8,128)(2,1)} copy(bf16[128,8,16,128]{3,1,2,0:T(8,128)(2,1)} %bitcast.23) | data formatting | bytes 8388608
  90.6 0.0 copy-done
  90.6 74.1 %while.11 = (s32[]{:T(128)}, bf16[2,8,1024,128]{2,3,1,0:T(8,128)(2,1)}, bf16[2,8,1024,128]{3,1,0,2:T(8,128)(2,1)}, bf16[2,1024,128]{2,1,0:T(8,128)(2,1)}, bf16[2...) while((s32[]{:T(128)}, bf16[2,8,1024,128]{2,3,1,0:T(8,128)(2,1)}, ...), condition=%wide.region_3.4_spmd.clone, body=%wide.region_0.3_spmd.clone.sunk | while | flops 4350542848 | bytes 54072912 | solution.py:37
  90.6 1.7 constant_dynamic-slice_fusion.2
  92.3 0.6 fusion.52
  92.9 20.1 %fusion.53 = (f32[8,1024]{1,0:T(8,128)S(1)}, bf16[8,1024,1024]{1,2,0:T(8,128)(2,1)}) fusion(pred[1024,1024]{0,1:T(8,128)(4,1)S(1)} %fusion.52, bf16[1,8,1024,128]{3,1,0,2:T(8,128)(2,1)S(1)} %constant_dynamic-slice_fusion.2, bf16[2,1024,128]{2,1,0:T(8,128)(2,1)} %get-tuple-element.134, s32[]{:T(128)} %get-tuple-element.124), kind=kOutput, calls=%fused_computation.37.clone.1 | convolution fusion | flops 2197816320 | bytes 21266944 | tf_op jit(solution)/shard_map/while/body/eval_jaxpr/sub | solution.py:28
  113.1 10.1 %fusion.54 = bf16[1,8,1024,128]{3,2,1,0:T(8,128)(2,1)} fusion(f32[8,1024]{1,0:T(8,128)S(1)} %get-tuple-element.115, bf16[8,1024,1024]{1,2,0:T(8,128)(2,1)} %get-tuple-element.116, bf16[2,1024,128]{2,1,0:T(8,128)(2,1)} %get-tuple-element.135, s32[]{:T(128)} %get-tuple-element.124), kind=kOutput, calls=%fused_computation.16.clone.1 | convolution fusion | flops 2149580800 | bytes 19169792 | tf_op jit(solution)/shard_map/while/body/eval_jaxpr/gqk,kd->gqd/dot_general | solution.py:32
  123.2 2.9 copy.46
  126.0 1.6 constant_dynamic-update-slice_fusion.2
  127.6 1.7 constant_dynamic-slice_fusion.2
  129.4 0.6 fusion.52
  130.0 20.1 %fusion.53 = (f32[8,1024]{1,0:T(8,128)S(1)}, bf16[8,1024,1024]{1,2,0:T(8,128)(2,1)}) fusion(pred[1024,1024]{0,1:T(8,128)(4,1)S(1)} %fusion.52, bf16[1,8,1024,128]{3,1,0,2:T(8,128)(2,1)S(1)} %constant_dynamic-slice_fusion.2, bf16[2,1024,128]{2,1,0:T(8,128)(2,1)} %get-tuple-element.134, s32[]{:T(128)} %get-tuple-element.124), kind=kOutput, calls=%fused_computation.37.clone.1 | convolution fusion | flops 2197816320 | bytes 21266944 | tf_op jit(solution)/shard_map/while/body/eval_jaxpr/sub | solution.py:28
  150.1 10.1 %fusion.54 = bf16[1,8,1024,128]{3,2,1,0:T(8,128)(2,1)} fusion(f32[8,1024]{1,0:T(8,128)S(1)} %get-tuple-element.115, bf16[8,1024,1024]{1,2,0:T(8,128)(2,1)} %get-tuple-element.116, bf16[2,1024,128]{2,1,0:T(8,128)(2,1)} %get-tuple-element.135, s32[]{:T(128)} %get-tuple-element.124), kind=kOutput, calls=%fused_computation.16.clone.1 | convolution fusion | flops 2149580800 | bytes 19169792 | tf_op jit(solution)/shard_map/while/body/eval_jaxpr/gqk,kd->gqd/dot_general | solution.py:32
  160.2 2.9 copy.46
  163.1 1.6 constant_dynamic-update-slice_fusion.2
  164.7 0.0 all-gather.3.cloned.1.call-update
  164.7 0.0 all-gather.5.cloned.1.call-start
  164.8 0.7 all-gather.5.cloned.1.call-update
  165.5 0.0 copy-start.1
  165.5 103.3 %all-gather.3.cloned.1.call-done = bf16[1024,4096]{0,1:T(8,128)(2,1)} async-done(((bf16[1024,2048]{0,1:T(8,128)(2,1)}), bf16[1024,4096]{0,1:T(8,128)(2,1)}) %all-gather.3.cloned.1.call-update) | async-done | bytes 8388624 | tf_op jit(solution)/shard_map/all_gather | solution.py:63
  268.8 169.7 %all-gather.5.cloned.1.call-done = bf16[4096,4096]{1,0:T(8,128)(2,1)} async-done(((bf16[256,4096]{1,0:T(8,128)(2,1)}), bf16[4096,4096]{1,0:T(8,128)(2,1)}) %all-gather.5.cloned.1.call-update) | async-done | bytes 33554448 | tf_op jit(solution)/shard_map/all_gather | solution.py:66
  438.5 45.1 %multiply_reduce_fusion = (f32[1024]{0:T(1024)S(1)}, f32[1024,4096]{1,0:T(8,128)}) fusion(bf16[1024,4096]{0,1:T(8,128)(2,1)} %all-gather.3.cloned.1.call-done, bf16[4096,4096]{1,0:T(8,128)(2,1)} %all-gather.5.cloned.1.call-done, bf16[1024,4096]{1,0:T(8,128)(2,1)} %param.14), kind=kOutput, calls=%fused_computation.31 | convolution fusion | flops 34376515584 | bytes 67112960 | tf_op jit(solution)/shard_map/dot_general | solution.py:64
  483.6 4.9 psum.7
  488.5 0.0 copy-done.1
  488.5 19.5 %multiply_convert_fusion = (bf16[1024,4096]{1,0:T(8,128)(2,1)}, bf16[1024,4096]{1,0:T(8,128)(2,1)}) fusion(f32[1024,4096]{1,0:T(8,128)} %get-tuple-element.73, f32[4096]{0:T(1024)S(1)} %copy-done.1, f32[1024]{0:T(1024)S(1)} %add_rsqrt_fusion), kind=kLoop, calls=%fused_computation.30 | loop fusion | flops 16777216 | bytes 33574912 | tf_op jit(solution)/shard_map/convert_element_type | solution.py:73
  (2 shorter events, 0.0 us)
Async XLA Ops:
  9.0 12.9 %all-to-all-start.1 = ((bf16[512,2,256]{2,0,1:T(8,128)(2,1)}), bf16[512,2,256]{2,0,1:T(8,128)(2,1)S(1)}, u32[]{:S(2)}, u32[]{:S(2)}) async-start(bf16[512,2,256]{2,0,1:T(8,128)(2,1)} %bitcast.59), calls=%async_computation.1 | async-start | bytes 1048576 | tf_op jit(solution)/shard_map/all_to_all | solution.py:59
  22.0 11.2 %all-to-all-start.2 = ((bf16[512,2,256]{2,0,1:T(8,128)(2,1)}), bf16[512,2,256]{2,0,1:T(8,128)(2,1)S(1)}, u32[]{:S(2)}, u32[]{:S(2)}) async-start(bf16[512,2,256]{2,0,1:T(8,128)(2,1)} %bitcast.58), calls=%async_computation.2 | async-start | bytes 1048576 | tf_op jit(solution)/shard_map/all_to_all | solution.py:60
  33.1 51.8 %all-to-all-start = ((bf16[512,2,2048]{2,0,1:T(8,128)(2,1)}), bf16[512,2,2048]{2,0,1:T(8,128)(2,1)}, u32[]{:S(2)}, u32[]{:S(2)}) async-start(bf16[512,2,2048]{2,0,1:T(8,128)(2,1)} %bitcast.71), calls=%async_computation | async-start | bytes 8388608 | tf_op jit(solution)/shard_map/all_to_all | solution.py:58
  38.8 51.8 %copy-start = (s32[1,1024]{1,0:T(1,128)S(1)}, s32[1,1024]{1,0:T(1,128)}, u32[]{:S(2)}) copy-start(s32[1,1024]{1,0:T(1,128)} %param.12) | copy-start | bytes 12292
  38.8 230.0 %all-gather.3.cloned.1.call-start = ((), (), s32[]{:S(2)}) async-start(), calls=%async_computation.3 | async-start | bytes 12582912 | tf_op jit(solution)/shard_map/all_gather | solution.py:63
  164.7 273.8 %all-gather.5.cloned.1.call-start = ((), (), s32[]{:S(2)}) async-start(), calls=%async_computation.4 | async-start | bytes 35651584 | tf_op jit(solution)/shard_map/all_gather | solution.py:66
  165.5 323.1 %copy-start.1 = (f32[4096]{0:T(1024)S(1)}, f32[4096]{0:T(1024)}, u32[]{:S(2)}) copy-start(f32[4096]{0:T(1024)} %param.15) | copy-start | bytes 49156
Sparse Core Ops, SparseCore 0:
  164.9 103.9 all-gather.2
  270.4 168.0 all-gather.4
where the time goes:
time: 516 us; the launch traced here: 515 us
  waiting for transfers between devices  328 us (64%)
  matrix products  106 us (21%)
  local copies, waits for them, and re-layouts  28.5 us (6%)
  other arithmetic  20.7 us (4%)
  between operations  14.1 us (3%)
  starting transfers between devices  13.4 us (3%)
    all_gather x1, waiting for transfers between devices, body(): lax.all_gather(out_weight, 'col', axis=0, tiled=True)  170 us
    all_gather x1, waiting for transfers between devices, body(): panel_rows = lax.all_gather(attn, 'row', axis=1, tiled=True)  103 us
    dot_general x1, matrix products, body(): jnp.dot(panel_rows, lax.all_gather(out_weight, 'col', axis=0, tiled=True)...  45.1 us
    all_to_all x1, waiting for transfers between devices, body(): lax.all_to_all(query_proj, 'row', split_axis=1, concat_axis=0, tiled=True)  44.1 us
    sub x2, matrix products, one_group(): weights = jnp.where(allowed, jnp.exp(scores - peak), jnp.float32(0.0))  40.3 us
    dot_general x2, matrix products, one_group(): jnp.einsum('gqk,kd->gqd', probs, group_value, preferred_element_type=jnp....  20.2 us
    convert_element_type x1, other arithmetic, body(): return (hidden_sum.astype(jnp.bfloat16), normed.astype(jnp.bfloat16))  19.5 us
  transfers between devices with their start and end apart: 5, of which 5 were waited for; matrix products, arithmetic and copies ran while one was open for 2% of the time, Pallas kernels for 0%

commit v1 on v0

--- a/solution.py
+++ b/solution.py
@@ -6,6 +6,28 @@
 D = 8192
 HD = 128
 HK = 4
+
+
+def in_order(blocks, dim):
+    shape = list(blocks.shape[1:])
+    shape[dim] *= blocks.shape[0]
+    return jnp.moveaxis(blocks, 0, dim).reshape(shape)
+
+
+def ring_gather(x, axis, dim):
+    count = lax.axis_size(axis)
+    pairs = [(i, (i + 1) % count) for i in range(count)]
+    back = [(b, a) for a, b in pairs]
+    lower, upper = ([], [])
+    for step in range(count - 1):
+        if step % 2 == 0:
+            lower.append(lax.ppermute(lower[-1] if lower else x, axis, pairs))
+        else:
+            upper.append(lax.ppermute(upper[-1] if upper else x, axis, back))
+    tiles = jnp.stack([*lower[::-1], x, *upper])
+    shift = lax.axis_index(axis) - len(lower)
+    tiles = tiles[(jnp.arange(count) - shift) % count]
+    return in_order(tiles, dim)
 
 
 def attend_local(query_heads, key_heads, value_heads, segment_row):
@@ -62,9 +84,7 @@
     attn = attend_local(query_heads, key_heads, value_heads, segment_ids[0])
     panel_rows = lax.all_gather(attn, "row", axis=1, tiled=True)
     projected = jnp.dot(
-        panel_rows,
-        lax.all_gather(out_weight, "col", axis=0, tiled=True),
-        preferred_element_type=jnp.float32,
+        panel_rows, ring_gather(out_weight, "col", 0), preferred_element_type=jnp.float32
     )
     hidden_sum = residual.astype(jnp.float32) + projected
     squares = lax.psum(jnp.sum(hidden_sum * hidden_sum, axis=1), "row")

time: 516 us -> 566 us (1.097)
  waiting for transfers between devices: 328 us -> 139 us
  starting transfers between devices: 13.4 us -> 161 us
  local copies, waits for them, and re-layouts: 28.5 us -> 96.4 us
  other arithmetic: 20.7 us -> 44.2 us
    all_gather x1 -> x0, waiting for transfers between devices: 170 us -> none  [body(): lax.all_gather(out_weight, 'col', axis=0, tiled=True)]
    ppermute x0 -> x15, starting transfers between devices: none -> 148 us  [the longest x8 140 us: ring_gather(): lower.append(lax.ppermute(lower[-1] if lower else x, axis, pairs))]
    all_gather x1, waiting for transfers between devices: 103 us -> 13.3 us  [body(): panel_rows = lax.all_gather(attn, 'row', axis=1, tiled=True)]
    ppermute x0 -> x15, waiting for transfers between devices: none -> 72.3 us  [the longest x8 70.7 us: ring_gather(): lower.append(lax.ppermute(lower[-1] if lower else x, axis, pairs))]
    gather x0 -> x3, local copies, waits for them, and re-layouts: none -> 38.1 us  [ring_gather(): tiles = tiles[(jnp.arange(count) - shift) % count]]
    unnamed x7 -> x44, local copies, waits for them, and re-layouts: 7.38 us -> 34.6 us
    unnamed x0 -> x1, other arithmetic: none -> 22.8 us
  transfers between devices with their start and end apart: 5 -> 19, of which waited for: 5 -> 10; matrix products, arithmetic and copies ran while one was open for 2% -> 31% of each run, Pallas kernels for 0% -> 0%
where the time goes in v1:
time: 566 us; the launch traced here: 565 us
  starting transfers between devices  161 us (28%)
  waiting for transfers between devices  139 us (25%)
  matrix products  106 us (19%)
  local copies, waits for them, and re-layouts  96.4 us (17%)
  other arithmetic  44.2 us (8%)
  between operations  14.4 us (3%)
    ppermute x8, starting transfers between devices, ring_gather(): lower.append(lax.ppermute(lower[-1] if lower else x, axis, pairs))  140 us
    ppermute x8, waiting for transfers between devices, ring_gather(): lower.append(lax.ppermute(lower[-1] if lower else x, axis, pairs))  70.7 us
    dot_general x1, matrix products, body(): jnp.dot(panel_rows, ring_gather(out_weight, 'col', 0), preferred_element_...  45.1 us
    all_to_all x1, waiting for transfers between devices, body(): lax.all_to_all(query_proj, 'row', split_axis=1, concat_axis=0, tiled=True)  43 us
    sub x2, matrix products, one_group(): weights = jnp.where(allowed, jnp.exp(scores - peak), jnp.float32(0.0))  40.3 us
    gather x3, local copies, waits for them, and re-layouts, ring_gather(): tiles = tiles[(jnp.arange(count) - shift) % count]  38.1 us
    unnamed x44, local copies, waits for them, and re-layouts  34.6 us
    unnamed x1, other arithmetic  22.8 us
  transfers between devices with their start and end apart: 19, of which 10 were waited for; matrix products, arithmetic and copies ran while one was open for 31% of the time, Pallas kernels for 0%

profile of v1, /device:TPU:0, one launch (start us, length us, event | category | flops | bytes accessed | tf_op | source)
XLA Modules:
  0.0 565.2 jit_solution(454964540189847443)
XLA Ops:
  7.2 0.5 collective-permute-start
  7.7 28.9 %collective-permute-done = bf16[256,4096]{1,0:T(8,128)(2,1)S(1)} collective-permute-done((bf16[256,4096]{1,0:T(8,128)(2,1)}, bf16[256,4096]{1,0:T(8,128)(2,1)S(1)}, u32[]{:S(2)}, u32[]{:S(2)}) %collective-permute-start) | collective-permute-done | bytes 2097184 | tf_op jit(solution)/shard_map/ppermute | solution.py:24
  36.6 1.3 copy-done.1
  37.9 4.4 collective-permute-start.8
  42.4 23.8 %collective-permute-done.1 = bf16[256,4096]{1,0:T(8,128)(2,1)S(1)} collective-permute-done((bf16[256,4096]{1,0:T(8,128)(2,1)S(1)}, bf16[256,4096]{1,0:T(8,128)(2,1)S(1)}, u32[]{:S(2)}, u32[]{:S(2)}) %collective-permute-start.1) | collective-permute-done | bytes 2097184 | tf_op jit(solution)/shard_map/ppermute | solution.py:24
  66.2 16.6 %collective-permute-start.2 = (bf16[256,4096]{1,0:T(8,128)(2,1)S(1)}, bf16[256,4096]{1,0:T(8,128)(2,1)S(1)}, u32[]{:S(2)}, u32[]{:S(2)}) collective-permute-start(bf16[256,4096]{1,0:T(8,128)(2,1)S(1)} %collective-permute-done.1), channel_id=1, source_target_pairs={{0,1},{1,2},{2,3},{3,4},{4,5},{5,6},{6,7},{7,8},{8,9},{9,10},{10,1... | collective-permute-start | bytes 6291464 | tf_op jit(solution)/shard_map/ppermute | solution.py:24
  82.8 1.3 copy-done.3
  84.1 10.4 %collective-permute-done.2 = bf16[256,4096]{1,0:T(8,128)(2,1)S(1)} collective-permute-done((bf16[256,4096]{1,0:T(8,128)(2,1)S(1)}, bf16[256,4096]{1,0:T(8,128)(2,1)S(1)}, u32[]{:S(2)}, u32[]{:S(2)}) %collective-permute-start.2) | collective-permute-done | bytes 2097184 | tf_op jit(solution)/shard_map/ppermute | solution.py:24
  94.5 36.2 %collective-permute-start.3 = (bf16[256,4096]{1,0:T(8,128)(2,1)S(1)}, bf16[256,4096]{1,0:T(8,128)(2,1)S(1)}, u32[]{:S(2)}, u32[]{:S(2)}) collective-permute-start(bf16[256,4096]{1,0:T(8,128)(2,1)S(1)} %collective-permute-done.2), channel_id=1, source_target_pairs={{0,1},{1,2},{2,3},{3,4},{4,5},{5,6},{6,7},{7,8},{8,9},{9,10},{10,1... | collective-permute-start | bytes 6291464 | tf_op jit(solution)/shard_map/ppermute | solution.py:24
  130.8 1.3 copy-done.7
  132.1 3.7 collective-permute-done.3
  135.8 42.1 %collective-permute-start.4 = (bf16[256,4096]{1,0:T(8,128)(2,1)S(1)}, bf16[256,4096]{1,0:T(8,128)(2,1)}, u32[]{:S(2)}, u32[]{:S(2)}) collective-permute-start(bf16[256,4096]{1,0:T(8,128)(2,1)S(1)} %collective-permute-done.3), channel_id=1, source_target_pairs={{0,1},{1,2},{2,3},{3,4},{4,5},{5,6},{6,7},{7,8},{8,9},{9,10},{10,1... | collective-permute-start | bytes 6291464 | tf_op jit(solution)/shard_map/ppermute | solution.py:24
  178.0 3.8 collective-permute-done.4
  181.8 43.3 %collective-permute-start.5 = (bf16[256,4096]{1,0:T(8,128)(2,1)}, bf16[256,4096]{1,0:T(8,128)(2,1)}, u32[]{:S(2)}, u32[]{:S(2)}) collective-permute-start(bf16[256,4096]{1,0:T(8,128)(2,1)} %collective-permute-done.4), channel_id=1, source_target_pairs={{0,1},{1,2},{2,3},{3,4},{4,5},{5,6},{6,7},{7,8},{8,9},{9,10},{10,1... | collective-permute-start | bytes 6291464 | tf_op jit(solution)/shard_map/ppermute | solution.py:24
  225.1 1.9 copy.42
  227.0 3.5 all-to-all-start.1
  230.5 1.9 copy.41
  232.4 5.8 %all-to-all-done.1 = bf16[512,2,256]{2,0,1:T(8,128)(2,1)S(1)} async-done(((bf16[512,2,256]{2,0,1:T(8,128)(2,1)}), bf16[512,2,256]{2,0,1:T(8,128)(2,1)S(1)}, u32[]{:S(2)}, u32[]{:S(2)}) %all-to-all-start.1) | async-done | bytes 524320 | tf_op jit(solution)/shard_map/all_to_all | solution.py:81
  238.2 3.5 all-to-all-start.2
  241.7 4.8 copy.40
  246.5 4.1 all-to-all-done.2
  250.6 5.6 all-to-all-start
  256.9 0.6 pad_clamp_fusion
  257.5 0.9 reshape.86
  258.4 1.9 copy.15
  260.5 0.9 copy.16
  261.3 43.0 %all-to-all-done = bf16[512,2,2048]{2,0,1:T(8,128)(2,1)} async-done(((bf16[512,2,2048]{2,0,1:T(8,128)(2,1)}), bf16[512,2,2048]{2,0,1:T(8,128)(2,1)}, u32[]{:S(2)}, u32[]{:S(2)}) %all-to-all-start) | async-done | bytes 4194336 | tf_op jit(solution)/shard_map/all_to_all | solution.py:80
  304.4 5.6 copy.25
  310.0 0.5 collective-permute-start.7
  310.5 74.3 %while.11 = (s32[]{:T(128)}, bf16[2,8,1024,128]{2,3,1,0:T(8,128)(2,1)}, bf16[2,8,1024,128]{3,1,0,2:T(8,128)(2,1)}, bf16[2,1024,128]{2,1,0:T(8,128)(2,1)}, bf16[2...) while((s32[]{:T(128)}, bf16[2,8,1024,128]{2,3,1,0:T(8,128)(2,1)}, ...), condition=%wide.region_3.4_spmd.clone, body=%wide.region_0.3_spmd.clone.sunk | while | flops 4350542848 | bytes 54072912 | solution.py:59
  310.5 1.7 constant_dynamic-slice_fusion.2
  312.2 0.6 fusion.55
  312.8 20.2 %fusion.56 = (f32[8,1024]{1,0:T(8,128)S(1)}, bf16[8,1024,1024]{1,2,0:T(8,128)(2,1)}) fusion(pred[1024,1024]{0,1:T(8,128)(4,1)S(1)} %fusion.55, bf16[1,8,1024,128]{3,1,0,2:T(8,128)(2,1)S(1)} %constant_dynamic-slice_fusion.2, bf16[2,1024,128]{2,1,0:T(8,128)(2,1)} %get-tuple-element.136, s32[]{:T(128)} %get-tuple-element.126), kind=kOutput, calls=%fused_computation.63.clone.1 | convolution fusion | flops 2197816320 | bytes 21266944 | tf_op jit(solution)/shard_map/while/body/eval_jaxpr/sub | solution.py:50
  333.0 10.2 %fusion.57 = bf16[1,8,1024,128]{3,2,1,0:T(8,128)(2,1)} fusion(f32[8,1024]{1,0:T(8,128)S(1)} %get-tuple-element.117, bf16[8,1024,1024]{1,2,0:T(8,128)(2,1)} %get-tuple-element.118, bf16[2,1024,128]{2,1,0:T(8,128)(2,1)} %get-tuple-element.137, s32[]{:T(128)} %get-tuple-element.126), kind=kOutput, calls=%fused_computation.18.clone.1 | convolution fusion | flops 2149580800 | bytes 19169792 | tf_op jit(solution)/shard_map/while/body/eval_jaxpr/gqk,kd->gqd/dot_general | solution.py:54
  343.2 2.9 copy.46
  346.0 1.6 constant_dynamic-update-slice_fusion.2
  347.6 1.7 constant_dynamic-slice_fusion.2
  349.4 0.6 fusion.55
  350.0 20.2 %fusion.56 = (f32[8,1024]{1,0:T(8,128)S(1)}, bf16[8,1024,1024]{1,2,0:T(8,128)(2,1)}) fusion(pred[1024,1024]{0,1:T(8,128)(4,1)S(1)} %fusion.55, bf16[1,8,1024,128]{3,1,0,2:T(8,128)(2,1)S(1)} %constant_dynamic-slice_fusion.2, bf16[2,1024,128]{2,1,0:T(8,128)(2,1)} %get-tuple-element.136, s32[]{:T(128)} %get-tuple-element.126), kind=kOutput, calls=%fused_computation.63.clone.1 | convolution fusion | flops 2197816320 | bytes 21266944 | tf_op jit(solution)/shard_map/while/body/eval_jaxpr/sub | solution.py:50
  370.1 10.2 %fusion.57 = bf16[1,8,1024,128]{3,2,1,0:T(8,128)(2,1)} fusion(f32[8,1024]{1,0:T(8,128)S(1)} %get-tuple-element.117, bf16[8,1024,1024]{1,2,0:T(8,128)(2,1)} %get-tuple-element.118, bf16[2,1024,128]{2,1,0:T(8,128)(2,1)} %get-tuple-element.137, s32[]{:T(128)} %get-tuple-element.126), kind=kOutput, calls=%fused_computation.18.clone.1 | convolution fusion | flops 2149580800 | bytes 19169792 | tf_op jit(solution)/shard_map/while/body/eval_jaxpr/gqk,kd->gqd/dot_general | solution.py:54
  380.3 2.9 copy.46
  383.2 1.6 constant_dynamic-update-slice_fusion.2
  384.8 4.1 collective-permute-start.14
  388.9 1.8 bitcast_dynamic-update-slice_fusion.15
  390.7 2.3 bitcast_dynamic-update-slice_fusion.14
  393.0 2.2 bitcast_dynamic-update-slice_fusion.13
  395.2 2.1 bitcast_dynamic-update-slice_fusion.12
  397.3 2.0 bitcast_dynamic-update-slice_fusion.11
  399.3 2.0 bitcast_dynamic-update-slice_fusion.10
  402.0 2.0 bitcast_dynamic-update-slice_fusion.5
  403.9 1.8 bitcast_dynamic-update-slice_fusion.4
  405.8 1.8 bitcast_dynamic-update-slice_fusion.3
  407.6 1.8 bitcast_dynamic-update-slice_fusion.2
  409.4 1.8 bitcast_dynamic-update-slice_fusion.1
  411.2 1.6 collective-permute-done.14
  412.8 1.8 bitcast_dynamic-update-slice_fusion
  414.6 11.7 %fusion.42 = (bf16[16,256,2048]{2,1,0:T(8,128)(2,1)}, bf16[16,256,2048]{2,1,0:T(8,128)(2,1)}) fusion(bf16[16,256,4096]{2,1,0:T(8,128)(2,1)S(1)} %bitcast_dynamic-update-slice_fusion), kind=kLoop, calls=%fused_computation.64 | loop fusion | bytes 67108864 | tf_op jit(solution)/shard_map/gather | solution.py:29
  426.3 13.2 %gather_fusion = bf16[16,256,2048]{2,1,0:T(8,128)(2,1)} fusion(bf16[16,256,2048]{2,1,0:T(8,128)(2,1)} %get-tuple-element.70, s32[1024]{0:T(1024)} %pad_clamp_fusion), kind=kCustom, calls=%fused_computation | custom fusion | bytes 33554496 | tf_op jit(solution)/shard_map/gather | solution.py:29
  439.5 13.2 %gather_fusion.1 = bf16[16,256,2048]{2,1,0:T(8,128)(2,1)} fusion(bf16[16,256,2048]{2,1,0:T(8,128)(2,1)} %get-tuple-element.71, s32[1024]{0:T(1024)} %pad_clamp_fusion), kind=kCustom, calls=%fused_computation.1 | custom fusion | bytes 33554496 | tf_op jit(solution)/shard_map/gather | solution.py:29
  452.6 22.8 %pad_maximum_fusion = bf16[16,256,4096]{2,1,0:T(8,128)(2,1)} fusion(bf16[16,256,2048]{2,1,0:T(8,128)(2,1)} %gather_fusion.1, bf16[16,256,2048]{2,1,0:T(8,128)(2,1)} %gather_fusion), kind=kLoop, calls=%fused_computation.32 | loop fusion | flops 67108864 | bytes 67108864
  475.4 13.3 %all-gather.2.cloned.1.call-done = bf16[1024,4096]{0,1:T(8,128)(2,1)} async-done(((bf16[1024,2048]{0,1:T(8,128)(2,1)}), bf16[1024,4096]{0,1:T(8,128)(2,1)}) %all-gather.2.cloned.1.call-update) | async-done | bytes 8388624 | tf_op jit(solution)/shard_map/all_gather | solution.py:85
  488.8 45.1 %multiply_reduce_fusion = (f32[1024]{0:T(1024)S(1)}, f32[1024,4096]{1,0:T(8,128)}) fusion(bf16[1024,4096]{0,1:T(8,128)(2,1)} %all-gather.2.cloned.1.call-done, bf16[4096,4096]{1,0:T(8,128)(2,1)} %bitcast.106, bf16[1024,4096]{1,0:T(8,128)(2,1)} %param.14), kind=kOutput, calls=%fused_computation.34 | convolution fusion | flops 34376515584 | bytes 67112960 | tf_op jit(solution)/shard_map/dot_general | solution.py:86
  533.9 4.9 psum.7
  538.8 19.6 %multiply_convert_fusion = (bf16[1024,4096]{1,0:T(8,128)(2,1)}, bf16[1024,4096]{1,0:T(8,128)(2,1)}) fusion(f32[1024,4096]{1,0:T(8,128)} %get-tuple-element.75, f32[4096]{0:T(1024)S(1)} %copy-done.12, f32[1024]{0:T(1024)S(1)} %add_rsqrt_fusion), kind=kLoop, calls=%fused_computation.33 | loop fusion | flops 16777216 | bytes 33574912 | tf_op jit(solution)/shard_map/convert_element_type | solution.py:93
  (49 shorter events, 1.5 us)
Async XLA Ops:
  7.2 29.4 %collective-permute-start = (bf16[256,4096]{1,0:T(8,128)(2,1)}, bf16[256,4096]{1,0:T(8,128)(2,1)S(1)}, u32[]{:S(2)}, u32[]{:S(2)}) collective-permute-start(bf16[256,4096]{1,0:T(8,128)(2,1)} %param.13), channel_id=1, source_target_pairs={{0,1},{1,2},{2,3},{3,4},{4,5},{5,6},{6,7},{7,8},{8,9},{9,10},{10,1... | collective-permute-start | bytes 6291464 | tf_op jit(solution)/shard_map/ppermute | solution.py:24
  36.6 1.4 copy-start.1
  37.9 28.3 %collective-permute-start.1 = (bf16[256,4096]{1,0:T(8,128)(2,1)S(1)}, bf16[256,4096]{1,0:T(8,128)(2,1)S(1)}, u32[]{:S(2)}, u32[]{:S(2)}) collective-permute-start(bf16[256,4096]{1,0:T(8,128)(2,1)S(1)} %collective-permute-done), channel_id=1, source_target_pairs={{0,1},{1,2},{2,3},{3,4},{4,5},{5,6},{6,7},{7,8},{8,9},{9,10},{10,1... | collective-permute-start | bytes 6291464 | tf_op jit(solution)/shard_map/ppermute | solution.py:24
  37.9 44.8 %collective-permute-start.8 = (bf16[256,4096]{1,0:T(8,128)(2,1)}, bf16[256,4096]{1,0:T(8,128)(2,1)S(1)}, u32[]{:S(2)}, u32[]{:S(2)}) collective-permute-start(bf16[256,4096]{1,0:T(8,128)(2,1)} %param.13), channel_id=1, source_target_pairs={{1,0},{2,1},{3,2},{4,3},{5,4},{6,5},{7,6},{8,7},{9,8},{10,9},{11,1... | collective-permute-start | bytes 6291464 | tf_op jit(solution)/shard_map/ppermute | solution.py:26
  66.2 64.5 %copy-start.5 = (bf16[256,4096]{1,0:T(8,128)(2,1)}, bf16[256,4096]{1,0:T(8,128)(2,1)S(1)}, u32[]{:S(2)}) copy-start(bf16[256,4096]{1,0:T(8,128)(2,1)S(1)} %collective-permute-done.1) | copy-start | bytes 6291460
  66.2 28.3 %collective-permute-start.2 = (bf16[256,4096]{1,0:T(8,128)(2,1)S(1)}, bf16[256,4096]{1,0:T(8,128)(2,1)S(1)}, u32[]{:S(2)}, u32[]{:S(2)}) collective-permute-start(bf16[256,4096]{1,0:T(8,128)(2,1)S(1)} %collective-permute-done.1), channel_id=1, source_target_pairs={{0,1},{1,2},{2,3},{3,4},{4,5},{5,6},{6,7},{7,8},{8,9},{9,10},{10,1... | collective-permute-start | bytes 6291464 | tf_op jit(solution)/shard_map/ppermute | solution.py:24
  82.8 1.3 copy-start.3
  84.1 46.6 %collective-permute-start.9 = (bf16[256,4096]{1,0:T(8,128)(2,1)S(1)}, bf16[256,4096]{1,0:T(8,128)(2,1)S(1)}, u32[]{:S(2)}, u32[]{:S(2)}) collective-permute-start(bf16[256,4096]{1,0:T(8,128)(2,1)S(1)} %collective-permute-done.8), channel_id=1, source_target_pairs={{1,0},{2,1},{3,2},{4,3},{5,4},{6,5},{7,6},{8,7},{9,8},{10,9},{11,1... | collective-permute-start | bytes 6291464 | tf_op jit(solution)/shard_map/ppermute | solution.py:26
  94.5 83.5 %copy-start.8 = (bf16[256,4096]{1,0:T(8,128)(2,1)}, bf16[256,4096]{1,0:T(8,128)(2,1)S(1)}, u32[]{:S(2)}) copy-start(bf16[256,4096]{1,0:T(8,128)(2,1)S(1)} %collective-permute-done.2) | copy-start | bytes 6291460
  94.5 41.3 %collective-permute-start.3 = (bf16[256,4096]{1,0:T(8,128)(2,1)S(1)}, bf16[256,4096]{1,0:T(8,128)(2,1)S(1)}, u32[]{:S(2)}, u32[]{:S(2)}) collective-permute-start(bf16[256,4096]{1,0:T(8,128)(2,1)S(1)} %collective-permute-done.2), channel_id=1, source_target_pairs={{0,1},{1,2},{2,3},{3,4},{4,5},{5,6},{6,7},{7,8},{8,9},{9,10},{10,1... | collective-permute-start | bytes 6291464 | tf_op jit(solution)/shard_map/ppermute | solution.py:24
  130.7 1.4 copy-start.7
  130.7 47.2 %collective-permute-start.10 = (bf16[256,4096]{1,0:T(8,128)(2,1)S(1)}, bf16[256,4096]{1,0:T(8,128)(2,1)S(1)}, u32[]{:S(2)}, u32[]{:S(2)}) collective-permute-start(bf16[256,4096]{1,0:T(8,128)(2,1)S(1)} %collective-permute-done.9), channel_id=1, source_target_pairs={{1,0},{2,1},{3,2},{4,3},{5,4},{6,5},{7,6},{8,7},{9,8},{10,9},{11,1... | collective-permute-start | bytes 6291464 | tf_op jit(solution)/shard_map/ppermute | solution.py:26
  135.8 42.2 %copy-start.10 = (bf16[256,4096]{1,0:T(8,128)(2,1)}, bf16[256,4096]{1,0:T(8,128)(2,1)S(1)}, u32[]{:S(2)}) copy-start(bf16[256,4096]{1,0:T(8,128)(2,1)S(1)} %collective-permute-done.3) | copy-start | bytes 6291460
  135.8 46.0 %collective-permute-start.4 = (bf16[256,4096]{1,0:T(8,128)(2,1)S(1)}, bf16[256,4096]{1,0:T(8,128)(2,1)}, u32[]{:S(2)}, u32[]{:S(2)}) collective-permute-start(bf16[256,4096]{1,0:T(8,128)(2,1)S(1)} %collective-permute-done.3), channel_id=1, source_target_pairs={{0,1},{1,2},{2,3},{3,4},{4,5},{5,6},{6,7},{7,8},{8,9},{9,10},{10,1... | collective-permute-start | bytes 6291464 | tf_op jit(solution)/shard_map/ppermute | solution.py:24
  177.9 132.0 %copy-start.9 = (bf16[256,4096]{1,0:T(8,128)(2,1)}, bf16[256,4096]{1,0:T(8,128)(2,1)S(1)}, u32[]{:S(2)}) copy-start(bf16[256,4096]{1,0:T(8,128)(2,1)S(1)} %collective-permute-done.10) | copy-start | bytes 6291460
  177.9 78.4 %collective-permute-start.11 = (bf16[256,4096]{1,0:T(8,128)(2,1)S(1)}, bf16[256,4096]{1,0:T(8,128)(2,1)}, u32[]{:S(2)}, u32[]{:S(2)}) collective-permute-start(bf16[256,4096]{1,0:T(8,128)(2,1)S(1)} %collective-permute-done.10), channel_id=1, source_target_pairs={{1,0},{2,1},{3,2},{4,3},{5,4},{6,5},{7,6},{8,7},{9,8},{10,9},{11,1... | collective-permute-start | bytes 6291464 | tf_op jit(solution)/shard_map/ppermute | solution.py:26
  181.8 74.5 %collective-permute-start.5 = (bf16[256,4096]{1,0:T(8,128)(2,1)}, bf16[256,4096]{1,0:T(8,128)(2,1)}, u32[]{:S(2)}, u32[]{:S(2)}) collective-permute-start(bf16[256,4096]{1,0:T(8,128)(2,1)} %collective-permute-done.4), channel_id=1, source_target_pairs={{0,1},{1,2},{2,3},{3,4},{4,5},{5,6},{6,7},{7,8},{8,9},{9,10},{10,1... | collective-permute-start | bytes 6291464 | tf_op jit(solution)/shard_map/ppermute | solution.py:24
  225.1 85.4 %copy-start.11 = (s32[1,1024]{1,0:T(1,128)S(1)}, s32[1,1024]{1,0:T(1,128)}, u32[]{:S(2)}) copy-start(s32[1,1024]{1,0:T(1,128)} %param.12) | copy-start | bytes 12292
  227.0 11.2 %all-to-all-start.1 = ((bf16[512,2,256]{2,0,1:T(8,128)(2,1)}), bf16[512,2,256]{2,0,1:T(8,128)(2,1)S(1)}, u32[]{:S(2)}, u32[]{:S(2)}) async-start(bf16[512,2,256]{2,0,1:T(8,128)(2,1)} %bitcast.94), calls=%async_computation.1 | async-start | bytes 1048576 | tf_op jit(solution)/shard_map/all_to_all | solution.py:81
  238.2 12.4 %all-to-all-start.2 = ((bf16[512,2,256]{2,0,1:T(8,128)(2,1)}), bf16[512,2,256]{2,0,1:T(8,128)(2,1)S(1)}, u32[]{:S(2)}, u32[]{:S(2)}) async-start(bf16[512,2,256]{2,0,1:T(8,128)(2,1)} %bitcast.112), calls=%async_computation.2 | async-start | bytes 1048576 | tf_op jit(solution)/shard_map/all_to_all | solution.py:82
  250.6 53.7 %all-to-all-start = ((bf16[512,2,2048]{2,0,1:T(8,128)(2,1)}), bf16[512,2,2048]{2,0,1:T(8,128)(2,1)}, u32[]{:S(2)}, u32[]{:S(2)}) async-start(bf16[512,2,2048]{2,0,1:T(8,128)(2,1)} %bitcast.107), calls=%async_computation | async-start | bytes 8388608 | tf_op jit(solution)/shard_map/all_to_all | solution.py:80
  256.2 232.5 %all-gather.2.cloned.1.call-start = ((), (), s32[]{:S(2)}) async-start(), calls=%async_computation.3 | async-start | bytes 12582912 | tf_op jit(solution)/shard_map/all_gather | solution.py:85
  256.3 53.7 %collective-permute-start.12 = (bf16[256,4096]{1,0:T(8,128)(2,1)}, bf16[256,4096]{1,0:T(8,128)(2,1)}, u32[]{:S(2)}, u32[]{:S(2)}) collective-permute-start(bf16[256,4096]{1,0:T(8,128)(2,1)} %collective-permute-done.11), channel_id=1, source_target_pairs={{1,0},{2,1},{3,2},{4,3},{5,4},{6,5},{7,6},{8,7},{9,8},{10,9},{11,1... | collective-permute-start | bytes 6291464 | tf_op jit(solution)/shard_map/ppermute | solution.py:26
  256.4 53.6 %collective-permute-start.6 = (bf16[256,4096]{1,0:T(8,128)(2,1)}, bf16[256,4096]{1,0:T(8,128)(2,1)}, u32[]{:S(2)}, u32[]{:S(2)}) collective-permute-start(bf16[256,4096]{1,0:T(8,128)(2,1)} %collective-permute-done.5), channel_id=1, source_target_pairs={{0,1},{1,2},{2,3},{3,4},{4,5},{5,6},{6,7},{7,8},{8,9},{9,10},{10,1... | collective-permute-start | bytes 6291464 | tf_op jit(solution)/shard_map/ppermute | solution.py:24
  310.0 74.9 %collective-permute-start.13 = (bf16[256,4096]{1,0:T(8,128)(2,1)}, bf16[256,4096]{1,0:T(8,128)(2,1)}, u32[]{:S(2)}, u32[]{:S(2)}) collective-permute-start(bf16[256,4096]{1,0:T(8,128)(2,1)} %collective-permute-done.12), channel_id=1, source_target_pairs={{1,0},{2,1},{3,2},{4,3},{5,4},{6,5},{7,6},{8,7},{9,8},{10,9},{11,1... | collective-permute-start | bytes 6291464 | tf_op jit(solution)/shard_map/ppermute | solution.py:26
  310.0 78.9 %collective-permute-start.7 = (bf16[256,4096]{1,0:T(8,128)(2,1)}, bf16[256,4096]{1,0:T(8,128)(2,1)}, u32[]{:S(2)}, u32[]{:S(2)}) collective-permute-start(bf16[256,4096]{1,0:T(8,128)(2,1)} %collective-permute-done.6), channel_id=1, source_target_pairs={{0,1},{1,2},{2,3},{3,4},{4,5},{5,6},{6,7},{7,8},{8,9},{9,10},{10,1... | collective-permute-start | bytes 6291464 | tf_op jit(solution)/shard_map/ppermute | solution.py:24
  384.8 16.5 %copy-start.6 = (bf16[256,4096]{1,0:T(8,128)(2,1)S(1)}, bf16[256,4096]{1,0:T(8,128)(2,1)}, u32[]{:S(2)}) copy-start(bf16[256,4096]{1,0:T(8,128)(2,1)} %copy-done.5) | copy-start | bytes 6291460
  384.8 16.7 %copy-start.2 = (bf16[256,4096]{1,0:T(8,128)(2,1)S(1)}, bf16[256,4096]{1,0:T(8,128)(2,1)}, u32[]{:S(2)}) copy-start(bf16[256,4096]{1,0:T(8,128)(2,1)} %copy-done.1) | copy-start | bytes 6291460
  384.8 16.8 %copy-start = (bf16[256,4096]{1,0:T(8,128)(2,1)S(1)}, bf16[256,4096]{1,0:T(8,128)(2,1)}, u32[]{:S(2)}) copy-start(bf16[256,4096]{1,0:T(8,128)(2,1)} %param.13) | copy-start | bytes 6291460
  384.8 27.9 %collective-permute-start.14 = (bf16[256,4096]{1,0:T(8,128)(2,1)}, bf16[256,4096]{1,0:T(8,128)(2,1)}, u32[]{:S(2)}, u32[]{:S(2)}) collective-permute-start(bf16[256,4096]{1,0:T(8,128)(2,1)} %collective-permute-done.13), channel_id=1, source_target_pairs={{1,0},{2,1},{3,2},{4,3},{5,4},{6,5},{7,6},{8,7},{9,8},{10,9},{11,1... | collective-permute-start | bytes 6291464 | tf_op jit(solution)/shard_map/ppermute | solution.py:26
  390.7 11.1 %copy-start.4 = (bf16[256,4096]{1,0:T(8,128)(2,1)S(1)}, bf16[256,4096]{1,0:T(8,128)(2,1)}, u32[]{:S(2)}) copy-start(bf16[256,4096]{1,0:T(8,128)(2,1)} %copy-done.3) | copy-start | bytes 6291460
  488.8 50.0 %copy-start.12 = (f32[4096]{0:T(1024)S(1)}, f32[4096]{0:T(1024)}, u32[]{:S(2)}) copy-start(f32[4096]{0:T(1024)} %param.15) | copy-start | bytes 49156
Sparse Core Ops, SparseCore 0:
  384.9 103.8 all-gather.1
